TPU v7x, 32 devices: a whole 2x2x4 slice. The times are simulated.
32 devices in a mesh: layer: 4 (over y, x), row: 2 (over core), col: 4 (over z).
Axes of the slice: x: 2, y: 2, z: 4, core: 2. Of those that a mesh axis runs over, the one named last changes fastest.
Arguments:
- blocks: bfloat16 [13, 512, 128, 128], P(None, ('row', 'col'), 'layer'), may hold values from -0.29882812 to 0.29882812
- presence: int32 [13, 512], P(None, ('row', 'col')), may hold values from 0 to 1, as said below
Outputs:
- purified: bfloat16 [13, 512, 128, 128], P(None, ('row', 'col'), 'layer')
Inputs may be any that keep to these rules, and one draw needn't show every extreme that they name: `presence`: the tile on offset 0 is present in every block row.
All inputs are finite; a program needn't handle non-finite values.
Results may differ from a plain program's by a relative error of at most 0.01.
Values may be sent and summed in bfloat16 or wider, within the bound.
A program may use at most 320 MiB of HBM per device.

v0:
```python
import jax
import jax.numpy as jnp
import numpy as np
from jax import lax
from jax.sharding import PartitionSpec as P

NBG = 512
BAND = 3
FAR = 160


def passed_along(block, axis, distance):
    devices = range(lax.axis_size(axis))
    route = [((i - distance) % len(devices), i) for i in devices]
    return lax.ppermute(block, axis, route)


def with_halo(block, sides, width):
    for axis, dim in sides:
        count = lax.axis_size(axis)
        forward = [(i, i + 1) for i in range(count - 1)]
        forward.append((count - 1, 0))
        backward = [(target, source) for source, target in forward]
        low = lax.ppermute(
            lax.slice_in_dim(block, block.shape[dim] - width, None, axis=dim), axis, forward
        )
        high = lax.ppermute(lax.slice_in_dim(block, 0, width, axis=dim), axis, backward)
        block = jnp.concatenate([low, block, high], axis=dim)
    return block


def offset_table():
    values = list(range(-BAND, BAND + 1))
    values = values + [FAR - 1, FAR, FAR + 1, -FAR - 1, -FAR, -FAR + 1]
    return [value % NBG for value in values]


def pair_table(offsets):
    by_target = []
    for target_index in range(len(offsets)):
        entries = []
        for left_index in range(len(offsets)):
            for right_index in range(len(offsets)):
                if (offsets[left_index] + offsets[right_index]) % NBG == offsets[target_index]:
                    entries.append((left_index, right_index))
        by_target.append(entries)
    return by_target


def fetch_far(source, offset, groups, local_rows):
    whole_steps, remainder = divmod(offset, local_rows)
    upper = passed_along(source[:, remainder:], ("row", "col"), -whole_steps % groups)
    if remainder == 0:
        return upper
    lower = passed_along(source[:, :remainder], ("row", "col"), (-whole_steps - 1) % groups)
    return jnp.concatenate([upper, lower], axis=1)


def per_device(blocks, presence):
    groups = lax.axis_size(("row", "col"))
    local_rows = blocks.shape[1]
    offsets = offset_table()
    by_target = pair_table(offsets)
    weight_mask = presence.astype(jnp.float32)[:, :, None, None]
    masked = blocks * presence.astype(jnp.bfloat16)[:, :, None, None]
    padded = with_halo(masked, ((("row", "col"), 1),), BAND)
    far_windows = {}
    for left_index in range(2 * BAND + 1, len(offsets)):
        needed = sorted(
            set(
                (
                    entry[1]
                    for target_list in by_target
                    for entry in target_list
                    if entry[0] == left_index
                )
            )
        )
        picked = jnp.take(masked, np.array(needed), axis=0)
        far_windows[left_index] = (
            fetch_far(picked, offsets[left_index], groups, local_rows),
            needed,
        )

    def right_piece(left_index, right_index):
        if left_index <= 2 * BAND:
            return padded[right_index, left_index : left_index + local_rows]
        window, needed = far_windows[left_index]
        return window[needed.index(right_index)]

    def product(left_tiles):
        totals = []
        for target_index in range(len(offsets)):
            pairs = by_target[target_index]
            lefts = jnp.concatenate(
                [left_tiles[left_index] for left_index, right_index in pairs], axis=2
            )
            rights = jnp.concatenate(
                [right_piece(left_index, right_index) for left_index, right_index in pairs], axis=1
            )
            totals.append(
                jnp.einsum("ixk,iky->ixy", lefts, rights, preferred_element_type=jnp.float32)
            )
        return jnp.stack(totals)

    left_first = lax.all_to_all(masked, "layer", split_axis=3, concat_axis=2, tiled=True)
    second = (
        lax.psum_scatter(product(left_first), "layer", scatter_dimension=2, tiled=True)
        * weight_mask
    ).astype(jnp.bfloat16)
    left_second = lax.all_to_all(second, "layer", split_axis=3, concat_axis=2, tiled=True)
    third = (
        lax.psum_scatter(
            product(left_second).astype(jnp.bfloat16), "layer", scatter_dimension=2, tiled=True
        ).astype(jnp.float32)
        * weight_mask
    )
    return (3.0 * second.astype(jnp.float32) - 2.0 * third).astype(jnp.bfloat16)


def solution(mesh):
    placed = (P(None, ("row", "col"), "layer", None), P(None, ("row", "col")))
    return jax.shard_map(
        per_device,
        mesh=mesh,
        in_specs=placed,
        out_specs=P(None, ("row", "col"), "layer", None),
        check_vma=False,
    )
```

profile of v0, /device:TPU:0, one launch (start us, length us, event | category | flops | bytes accessed | tf_op | source)
XLA Modules:
  0.0 2231.8 jit_solution(13494582447131702137)
XLA Ops:
  7.9 6.6 broadcast_multiply_fusion
  14.5 24.0 %copy.159 = bf16[13,64,32,128]{1,2,0,3:T(8,128)(2,1)} copy(bf16[13,64,32,128]{3,2,1,0:T(8,128)(2,1)} %broadcast_multiply_fusion) | data formatting | bytes 13631488 | tf_op jit(solution)/shard_map/mul | solution.py:65
  38.5 13.8 reshape.119
  52.3 5.5 all-to-all-start
  79.5 5.6 gather_fusion.5
  105.4 5.9 gather_fusion
  134.3 111.9 %collective-permute-done.10 = bf16[6,31,32,128]{3,2,1,0:T(8,128)(2,1)} collective-permute-done((bf16[6,31,32,128]{3,2,1,0:T(8,128)(2,1)}, bf16[6,31,32,128]{3,2,1,0:T(8,128)(2,1)}, u32[]{:S(2)}, u32[]{:S(2)}) %collective-permute-start.10) | collective-permute-done | bytes 1523744 | tf_op jit(solution)/shard_map/ppermute | solution.py:15
  246.2 32.9 %collective-permute-start.4 = (bf16[6,33,32,128]{3,2,1,0:T(8,128)(2,1)S(1)}, bf16[6,33,32,128]{3,2,1,0:T(8,128)(2,1)S(1)}, u32[]{:S(2)}, u32[]{:S(2)}) collective-permute-start(bf16[6,33,32,128]{3,2,1,0:T(8,128)(2,1)S(1)} %copy-done.32), channel_id=1, source_target_pairs={{5,0},{6,1},{7,2},{0,3},{1,4},{2,5},{3,6},{4,7},{13,8},{14,9},{15,... | collective-permute-start | bytes 4866056 | tf_op jit(solution)/shard_map/ppermute | solution.py:15
  294.4 120.7 %collective-permute-start.2 = (bf16[6,33,32,128]{3,2,1,0:T(8,128)(2,1)S(1)}, bf16[6,33,32,128]{3,2,1,0:T(8,128)(2,1)}, u32[]{:S(2)}, u32[]{:S(2)}) collective-permute-start(bf16[6,33,32,128]{3,2,1,0:T(8,128)(2,1)S(1)} %slice.876), channel_id=1, source_target_pairs={{2,0},{3,1},{4,2},{5,3},{6,4},{7,5},{0,6},{1,7},{10,8},{11,9},{12,... | collective-permute-start | bytes 4866056 | tf_op jit(solution)/shard_map/ppermute | solution.py:15
  417.0 97.6 %collective-permute-done.9 = bf16[6,32,32,128]{3,2,1,0:T(8,128)(2,1)S(1)} collective-permute-done((bf16[6,32,32,128]{3,2,1,0:T(8,128)(2,1)S(1)}, bf16[6,32,32,128]{3,2,1,0:T(8,128)(2,1)S(1)}, u32[]{:S(2)}, u32[]{:S(2)}) %collective-permute-start.9) | collective-permute-done | bytes 1572896 | tf_op jit(solution)/shard_map/ppermute | solution.py:15
  523.1 93.8 %collective-permute-done.5 = bf16[6,31,32,128]{3,2,1,0:T(8,128)(2,1)} collective-permute-done((bf16[6,31,32,128]{3,2,1,0:T(8,128)(2,1)}, bf16[6,31,32,128]{3,2,1,0:T(8,128)(2,1)}, u32[]{:S(2)}, u32[]{:S(2)}) %collective-permute-start.5) | collective-permute-done | bytes 1523744 | tf_op jit(solution)/shard_map/ppermute | solution.py:15
  618.6 33.1 %collective-permute-done.2 = bf16[6,33,32,128]{3,2,1,0:T(8,128)(2,1)} collective-permute-done((bf16[6,33,32,128]{3,2,1,0:T(8,128)(2,1)S(1)}, bf16[6,33,32,128]{3,2,1,0:T(8,128)(2,1)}, u32[]{:S(2)}, u32[]{:S(2)}) %collective-permute-start.2) | collective-permute-done | bytes 1622048 | tf_op jit(solution)/shard_map/ppermute | solution.py:15
  655.7 30.6 %collective-permute-done.13 = bf16[6,33,32,128]{3,2,1,0:T(8,128)(2,1)S(1)} collective-permute-done((bf16[6,33,32,128]{3,2,1,0:T(8,128)(2,1)S(1)}, bf16[6,33,32,128]{3,2,1,0:T(8,128)(2,1)S(1)}, u32[]{:S(2)}, u32[]{:S(2)}) %collective-permute-start.13) | collective-permute-done | bytes 1622048 | tf_op jit(solution)/shard_map/ppermute | solution.py:15
  701.1 13.7 reshape.120
  714.8 13.1 copy.160
  746.8 4.9 copy.161
  756.6 5.1 copy.166
  795.0 15.4 concatenate.198
  810.4 21.3 concatenate.203
  831.7 26.5 %concatenate.207 = bf16[64,128,416]{2,1,0:T(8,128)(2,1)} concatenate(bf16[64,128,32]{2,1,0:T(8,128)(2,1)} %bitcast.600, bf16[64,128,32]{2,1,0:T(8,128)(2,1)} %bitcast.496, bf16[64,128,32]{2,1,0:T(8,128)(2,1)} %bitcast.472, bf16[64,128,32]{2,1,0:T(8,128)(2,1)S(1)} %bitcast.429, bf16[64,128,32]{2,1,0:T(8,128)(2,1)} %bitcast.452, bf16[64,128,32]{2,1,0:T(8,128)(2,1)} %bitcast.488, ...), dimensions={2} | concatenate | bytes 13631488 | tf_op jit(solution)/shard_map/concatenate | solution.py:95
  858.2 21.3 concatenate.211
  879.5 15.5 concatenate.213
  895.0 13.6 concatenate.217
  908.6 13.2 concatenate.219
  921.8 13.2 concatenate.221
  935.0 13.2 concatenate.223
  948.1 13.2 concatenate.225
  961.3 13.3 concatenate.227
  974.6 8.0 bitcast_dynamic-update-slice_fusion.12
  982.5 5.5 bitcast_dynamic-update-slice_fusion.11
  988.0 8.3 bitcast_dynamic-update-slice_fusion.10
  996.3 7.4 bitcast_dynamic-update-slice_fusion.9
  1003.7 6.4 bitcast_dynamic-update-slice_fusion.8
  1010.2 5.5 bitcast_dynamic-update-slice_fusion.7
  1032.8 5.4 bitcast_dynamic-update-slice_fusion.2
  1038.2 5.2 bitcast_dynamic-update-slice_fusion.1
  1043.4 5.1 bitcast_dynamic-update-slice_fusion
  1048.6 457.3 %reduce-scatter.3.cloned.1.call-done = f32[13,64,32,128]{3,2,1,0:T(8,128)} async-done(((f32[13,64,128,128]{3,2,1,0:T(8,128)}), f32[13,64,32,128]{3,2,1,0:T(8,128)}) %reduce-scatter.3.cloned.1.call-update) | async-done | bytes 13631504 | tf_op jit(solution)/shard_map/reduce_scatter | solution.py:108
  1505.9 8.1 multiply_convert_fusion
  1514.0 24.0 %copy.185 = bf16[13,64,32,128]{1,2,0,3:T(8,128)(2,1)} copy(bf16[13,64,32,128]{3,2,1,0:T(8,128)(2,1)} %multiply_convert_fusion) | data formatting | bytes 13631488 | tf_op jit(solution)/shard_map/convert_element_type | solution.py:110
  1538.1 13.8 reshape.121
  1551.9 83.3 %all_to_all.30 = bf16[4,2,425984]{2,1,0:T(2,128)(2,1)} all-to-all(bf16[4,2,425984]{2,1,0:T(2,128)(2,1)} %reshape.121), channel_id=1, replica_groups=mesh['layer'=4,'row'=2,'col'=4] {'layer'}, dimensions={0} | all-to-all | bytes 13631488 | tf_op jit(solution)/shard_map/all_to_all | solution.py:111
  1635.2 13.5 reshape.122
  1648.7 13.1 copy.186
  1690.5 5.1 copy.192
  1700.4 4.9 copy.195
  1728.8 7.4 bitcast_dynamic-update-slice_fusion.25
  1736.3 15.4 concatenate.230
  1751.7 21.3 concatenate.231
  1773.0 26.5 %concatenate.232 = bf16[64,128,416]{2,1,0:T(8,128)(2,1)} concatenate(bf16[64,128,32]{2,1,0:T(8,128)(2,1)} %bitcast.605, bf16[64,128,32]{2,1,0:T(8,128)(2,1)} %bitcast.504, bf16[64,128,32]{2,1,0:T(8,128)(2,1)} %bitcast.463, bf16[64,128,32]{2,1,0:T(8,128)(2,1)S(1)} %bitcast.417, bf16[64,128,32]{2,1,0:T(8,128)(2,1)} %bitcast.442, bf16[64,128,32]{2,1,0:T(8,128)(2,1)} %bitcast.481, ...), dimensions={2} | concatenate | bytes 13631488 | tf_op jit(solution)/shard_map/concatenate | solution.py:95
  1799.5 21.3 concatenate.233
  1820.8 15.5 concatenate.234
  1836.3 13.2 concatenate.236
  1849.5 13.2 concatenate.237
  1862.7 13.2 concatenate.238
  1875.9 13.2 concatenate.239
  1889.0 13.2 concatenate.240
  1902.2 13.4 concatenate.241
  1915.6 6.0 bitcast_dynamic-update-slice_fusion.24
  1921.7 7.6 bitcast_dynamic-update-slice_fusion.23
  1929.2 6.9 bitcast_dynamic-update-slice_fusion.22
  1936.2 5.8 bitcast_dynamic-update-slice_fusion.21
  1975.5 238.3 %reduce-scatter.5.cloned.1.call-done = bf16[13,64,32,128]{3,2,1,0:T(8,128)(2,1)} async-done(((bf16[13,64,128,128]{3,2,1,0:T(8,128)(2,1)}), bf16[13,64,32,128]{3,2,1,0:T(8,128)(2,1)}) %reduce-scatter.5.cloned.1.call-update) | async-done | bytes 6815760 | tf_op jit(solution)/shard_map/reduce_scatter | solution.py:113
  2213.9 10.7 subtract_convert_fusion
  (256 shorter events, 277.0 us)
Async XLA Ops:
  52.3 12.0 copy-start.58
  52.3 12.0 copy-start.59
  52.3 648.8 %all-to-all-start = ((bf16[4,2,425984]{2,1,0:T(2,128)(2,1)}), bf16[4,2,425984]{2,1,0:T(2,128)(2,1)}, u32[]{:S(2)}, u32[]{:S(2)}) async-start(bf16[4,2,425984]{2,1,0:T(2,128)(2,1)} %reshape.119), calls=%async_computation | async-start | bytes 13631488 | tf_op jit(solution)/shard_map/all_to_all | solution.py:106
  57.7 1448.2 %reduce-scatter.3.cloned.1.call-start = ((), (), s32[]{:S(2)}) async-start(), calls=%async_computation.4 | async-start | bytes 68157440 | tf_op jit(solution)/shard_map/reduce_scatter | solution.py:108
  59.7 67.6 %collective-permute-start.1 = (bf16[13,3,32,128]{3,2,1,0:T(8,128)(2,1)}, bf16[13,3,32,128]{3,2,1,0:T(8,128)(2,1)S(1)}, u32[]{:S(2)}, u32[]{:S(2)}) collective-permute-start(bf16[13,3,32,128]{3,2,1,0:T(8,128)(2,1)} %get-tuple-element.88), channel_id=1, source_target_pairs={{1,0},{2,1},{3,2},{4,3},{5,4},{6,5},{7,6},{0,7},{9,8},{10,9},{11,1... | collective-permute-start | bytes 958472 | tf_op jit(solution)/shard_map/ppermute | solution.py:27
  64.3 54.9 %collective-permute-start = (bf16[13,3,32,128]{3,2,1,0:T(8,128)(2,1)}, bf16[13,3,32,128]{3,2,1,0:T(8,128)(2,1)}, u32[]{:S(2)}, u32[]{:S(2)}) collective-permute-start(bf16[13,3,32,128]{3,2,1,0:T(8,128)(2,1)} %get-tuple-element.89), channel_id=1, source_target_pairs={{0,1},{1,2},{2,3},{3,4},{4,5},{5,6},{6,7},{7,0},{8,9},{9,10},{10,1... | collective-permute-start | bytes 958472 | tf_op jit(solution)/shard_map/ppermute | solution.py:24
  70.8 216.8 %collective-permute-start.6 = (bf16[6,32,32,128]{3,2,1,0:T(8,128)(2,1)}, bf16[6,32,32,128]{3,2,1,0:T(8,128)(2,1)}, u32[]{:S(2)}, u32[]{:S(2)}) collective-permute-start(bf16[6,32,32,128]{3,2,1,0:T(8,128)(2,1)} %get-tuple-element.129), channel_id=1, source_target_pairs={{2,0},{3,1},{4,2},{5,3},{6,4},{7,5},{0,6},{1,7},{10,8},{11,9},{12,... | collective-permute-start | bytes 4718600 | tf_op jit(solution)/shard_map/ppermute | solution.py:15
  75.3 9.9 copy-start.30
  77.1 169.1 %collective-permute-start.10 = (bf16[6,31,32,128]{3,2,1,0:T(8,128)(2,1)}, bf16[6,31,32,128]{3,2,1,0:T(8,128)(2,1)}, u32[]{:S(2)}, u32[]{:S(2)}) collective-permute-start(bf16[6,31,32,128]{3,2,1,0:T(8,128)(2,1)} %slice.922), channel_id=1, source_target_pairs={{2,0},{3,1},{4,2},{5,3},{6,4},{7,5},{0,6},{1,7},{10,8},{11,9},{12,... | collective-permute-start | bytes 4571144 | tf_op jit(solution)/shard_map/ppermute | solution.py:15
  88.0 191.1 %collective-permute-start.12 = (bf16[6,31,32,128]{3,2,1,0:T(8,128)(2,1)}, bf16[6,31,32,128]{3,2,1,0:T(8,128)(2,1)}, u32[]{:S(2)}, u32[]{:S(2)}) collective-permute-start(bf16[6,31,32,128]{3,2,1,0:T(8,128)(2,1)} %slice.927), channel_id=1, source_target_pairs={{5,0},{6,1},{7,2},{0,3},{1,4},{2,5},{3,6},{4,7},{13,8},{14,9},{15,... | collective-permute-start | bytes 4571144 | tf_op jit(solution)/shard_map/ppermute | solution.py:15
  105.4 13.0 slice-start
  111.3 6.7 copy-start.31
  111.3 7.1 slice-start.1
  119.2 175.2 %collective-permute-start.7 = (bf16[6,32,32,128]{3,2,1,0:T(8,128)(2,1)S(1)}, bf16[6,32,32,128]{3,2,1,0:T(8,128)(2,1)S(1)}, u32[]{:S(2)}, u32[]{:S(2)}) collective-permute-start(bf16[6,32,32,128]{3,2,1,0:T(8,128)(2,1)S(1)} %copy-done.39), channel_id=1, source_target_pairs={{3,0},{4,1},{5,2},{6,3},{7,4},{0,5},{1,6},{2,7},{11,8},{12,9},{13,... | collective-permute-start | bytes 4718600 | tf_op jit(solution)/shard_map/ppermute | solution.py:15
  127.3 287.8 %collective-permute-start.8 = (bf16[6,32,32,128]{3,2,1,0:T(8,128)(2,1)S(1)}, bf16[6,32,32,128]{3,2,1,0:T(8,128)(2,1)S(1)}, u32[]{:S(2)}, u32[]{:S(2)}) collective-permute-start(bf16[6,32,32,128]{3,2,1,0:T(8,128)(2,1)S(1)} %copy-done.41), channel_id=1, source_target_pairs={{5,0},{6,1},{7,2},{0,3},{1,4},{2,5},{3,6},{4,7},{13,8},{14,9},{15,... | collective-permute-start | bytes 4718600 | tf_op jit(solution)/shard_map/ppermute | solution.py:15
  131.2 115.0 %copy-start.32 = (bf16[6,33,32,128]{3,2,1,0:T(8,128)(2,1)S(1)}, bf16[6,33,32,128]{3,2,1,0:T(8,128)(2,1)}, u32[]{:S(2)}) copy-start(bf16[6,33,32,128]{3,2,1,0:T(8,128)(2,1)} %slice.879) | copy-start | bytes 4866052
  131.2 147.9 %copy-start.40 = (bf16[6,32,32,128]{3,2,1,0:T(8,128)(2,1)S(1)}, bf16[6,32,32,128]{3,2,1,0:T(8,128)(2,1)}, u32[]{:S(2)}) copy-start(bf16[6,32,32,128]{3,2,1,0:T(8,128)(2,1)} %get-tuple-element.126) | copy-start | bytes 4718596
  246.2 269.4 %collective-permute-start.4 = (bf16[6,33,32,128]{3,2,1,0:T(8,128)(2,1)S(1)}, bf16[6,33,32,128]{3,2,1,0:T(8,128)(2,1)S(1)}, u32[]{:S(2)}, u32[]{:S(2)}) collective-permute-start(bf16[6,33,32,128]{3,2,1,0:T(8,128)(2,1)S(1)} %copy-done.32), channel_id=1, source_target_pairs={{5,0},{6,1},{7,2},{0,3},{1,4},{2,5},{3,6},{4,7},{13,8},{14,9},{15,... | collective-permute-start | bytes 4866056 | tf_op jit(solution)/shard_map/ppermute | solution.py:15
  279.1 235.5 %collective-permute-start.9 = (bf16[6,32,32,128]{3,2,1,0:T(8,128)(2,1)S(1)}, bf16[6,32,32,128]{3,2,1,0:T(8,128)(2,1)S(1)}, u32[]{:S(2)}, u32[]{:S(2)}) collective-permute-start(bf16[6,32,32,128]{3,2,1,0:T(8,128)(2,1)S(1)} %copy-done.40), channel_id=1, source_target_pairs={{6,0},{7,1},{0,2},{1,3},{2,4},{3,5},{4,6},{5,7},{14,8},{15,9},{8,1... | collective-permute-start | bytes 4718600 | tf_op jit(solution)/shard_map/ppermute | solution.py:15
  287.6 329.3 %collective-permute-start.5 = (bf16[6,31,32,128]{3,2,1,0:T(8,128)(2,1)}, bf16[6,31,32,128]{3,2,1,0:T(8,128)(2,1)}, u32[]{:S(2)}, u32[]{:S(2)}) collective-permute-start(bf16[6,31,32,128]{3,2,1,0:T(8,128)(2,1)} %slice.880), channel_id=1, source_target_pairs={{6,0},{7,1},{0,2},{1,3},{2,4},{3,5},{4,6},{5,7},{14,8},{15,9},{8,1... | collective-permute-start | bytes 4571144 | tf_op jit(solution)/shard_map/ppermute | solution.py:15
  294.4 122.6 %copy-start.33 = (bf16[6,32,32,128]{3,2,1,0:T(8,128)(2,1)}, bf16[6,32,32,128]{3,2,1,0:T(8,128)(2,1)S(1)}, u32[]{:S(2)}) copy-start(bf16[6,32,32,128]{3,2,1,0:T(8,128)(2,1)S(1)} %collective-permute-done.7) | copy-start | bytes 4718596
  294.4 357.3 %collective-permute-start.2 = (bf16[6,33,32,128]{3,2,1,0:T(8,128)(2,1)S(1)}, bf16[6,33,32,128]{3,2,1,0:T(8,128)(2,1)}, u32[]{:S(2)}, u32[]{:S(2)}) collective-permute-start(bf16[6,33,32,128]{3,2,1,0:T(8,128)(2,1)S(1)} %slice.876), channel_id=1, source_target_pairs={{2,0},{3,1},{4,2},{5,3},{6,4},{7,5},{0,6},{1,7},{10,8},{11,9},{12,... | collective-permute-start | bytes 4866056 | tf_op jit(solution)/shard_map/ppermute | solution.py:15
  415.1 238.4 %collective-permute-start.3 = (bf16[6,31,32,128]{3,2,1,0:T(8,128)(2,1)}, bf16[6,31,32,128]{3,2,1,0:T(8,128)(2,1)}, u32[]{:S(2)}, u32[]{:S(2)}) collective-permute-start(bf16[6,31,32,128]{3,2,1,0:T(8,128)(2,1)} %slice.877), channel_id=1, source_target_pairs={{3,0},{4,1},{5,2},{6,3},{7,4},{0,5},{1,6},{2,7},{11,8},{12,9},{13,... | collective-permute-start | bytes 4571144 | tf_op jit(solution)/shard_map/ppermute | solution.py:15
  514.6 140.6 %collective-permute-start.11 = (bf16[6,33,32,128]{3,2,1,0:T(8,128)(2,1)S(1)}, bf16[6,33,32,128]{3,2,1,0:T(8,128)(2,1)S(1)}, u32[]{:S(2)}, u32[]{:S(2)}) collective-permute-start(bf16[6,33,32,128]{3,2,1,0:T(8,128)(2,1)S(1)} %slice.923), channel_id=1, source_target_pairs={{3,0},{4,1},{5,2},{6,3},{7,4},{0,5},{1,6},{2,7},{11,8},{12,9},{13,... | collective-permute-start | bytes 4866056 | tf_op jit(solution)/shard_map/ppermute | solution.py:15
  515.6 5.9 copy-start.36
  515.6 170.7 %collective-permute-start.13 = (bf16[6,33,32,128]{3,2,1,0:T(8,128)(2,1)S(1)}, bf16[6,33,32,128]{3,2,1,0:T(8,128)(2,1)S(1)}, u32[]{:S(2)}, u32[]{:S(2)}) collective-permute-start(bf16[6,33,32,128]{3,2,1,0:T(8,128)(2,1)S(1)} %slice.928), channel_id=1, source_target_pairs={{6,0},{7,1},{0,2},{1,3},{2,4},{3,5},{4,6},{5,7},{14,8},{15,9},{8,1... | collective-permute-start | bytes 4866056 | tf_op jit(solution)/shard_map/ppermute | solution.py:15
  693.1 5.6 copy-start.21
  693.1 5.6 copy-start.24
  693.1 5.6 copy-start.27
  961.3 13.3 copy-start.50
  961.3 13.3 copy-start.51
  974.6 8.0 copy-start.7
  982.5 13.7 slice-start.2
  988.0 8.3 slice-start.3
  988.0 15.7 slice-start.4
  996.3 7.4 slice-start.5
  1003.7 6.4 copy-start.6
  1010.1 5.6 copy-start.1
  1010.1 5.6 copy-start.3
  1010.1 5.6 copy-start.5
  1010.1 5.6 copy-start.42
  1010.1 5.6 copy-start.44
  1010.2 5.6 copy-start.46
  1010.2 5.6 copy-start.48
  1020.2 4.7 copy-start.25
  1032.8 5.4 copy-start.16
  1038.2 5.2 copy-start.15
  1048.5 457.4 %copy-start.52 = (f32[13,64]{1,0:T(8,128)S(1)}, f32[13,64]{1,0:T(8,128)}, u32[]{:S(2)}) copy-start(f32[13,64]{1,0:T(8,128)} %get-tuple-element.130) | copy-start | bytes 9988
  1048.5 1165.4 %reduce-scatter.5.cloned.1.call-start = ((), (), s32[]{:S(2)}) async-start(), calls=%async_computation.5 | async-start | bytes 34078720 | tf_op jit(solution)/shard_map/reduce_scatter | solution.py:113
  1915.6 13.6 slice-start.8
  1921.7 7.6 slice-start.9
  1921.7 14.5 slice-start.6
  1929.2 6.9 slice-start.7
  1936.2 5.8 copy-start.14
  1942.0 4.9 copy-start
  1942.0 4.9 copy-start.2
  1942.0 4.9 copy-start.4
  1942.0 4.9 copy-start.43
  1942.0 4.9 copy-start.45
  1942.0 4.9 copy-start.47
  1942.0 4.9 copy-start.49
  1961.6 4.7 copy-start.9
  1966.3 4.7 copy-start.8
  1975.5 238.4 %copy-start.53 = (f32[13,64]{1,0:T(8,128)S(1)}, f32[13,64]{1,0:T(8,128)}, u32[]{:S(2)}) copy-start(f32[13,64]{1,0:T(8,128)} %get-tuple-element.130) | copy-start | bytes 9988
  (23 other events, 75.9 us)
Sparse Core Ops, SparseCore 0:
  1048.6 457.2 reduce-scatter.2
  1975.7 238.1 reduce-scatter.4
where the time goes:
time: 2250 us; the launch traced here: 2230 us
  waiting for transfers between devices  1060 us (47%)
  local copies, waits for them, and re-layouts  707 us (31%)
  starting transfers between devices  179 us (8%)
  matrix products  136 us (6%)
  blocking collectives  83.3 us (4%)
  other arithmetic  49.6 us (2%)
    reduce_scatter x1, waiting for transfers between devices, per_device(): lax.psum_scatter(product(left_first), 'layer', scatter_dimension=2, tiled...  457 us
    ppermute x12, waiting for transfers between devices, passed_along(): return lax.ppermute(block, axis, route)  367 us
    concatenate x22, local copies, waits for them, and re-layouts, product(): jnp.concatenate([left_tiles[left_index] for left_index, right_index in pa...  359 us
    reduce_scatter x1, waiting for transfers between devices, per_device(): lax.psum_scatter(product(left_second).astype(jnp.bfloat16), 'layer', scat...  238 us
    ppermute x12, starting transfers between devices, passed_along(): return lax.ppermute(block, axis, route)  169 us
    dot_general x26, matrix products, product(): jnp.einsum('ixk,iky->ixy', lefts, rights, preferred_element_type=jnp.floa...  136 us
    slice x28, local copies, waits for them, and re-layouts, product(): left_tiles[left_index]  134 us
    all_to_all x1, blocking collectives, per_device(): lax.all_to_all(second, 'layer', split_axis=3, concat_axis=2, tiled=True)  83.3 us
  transfers between devices with their start and end apart: 17, of which 7 were waited for; matrix products, arithmetic and copies ran while one was open for 5% of the time, Pallas kernels for 0%

commit v1 on v0

v1 whole, which is shorter than its diff:
```python
import functools

import jax
import jax.numpy as jnp
from jax import lax
from jax.experimental import pallas as pl
from jax.experimental.pallas import tpu as pltpu
from jax.sharding import PartitionSpec as P

BAND = 3
FAR = 160
WIDTH = 2 * BAND + 1
MESH = pl.DeviceIdType.MESH


def offset_table(total_rows):
    values = list(range(-BAND, BAND + 1))
    values = values + [FAR - 1, FAR, FAR + 1, -FAR - 1, -FAR, -FAR + 1]
    return [value % total_rows for value in values]


def pair_table(offsets, total_rows):
    by_target = []
    for target in offsets:
        entries = []
        for left_index, left in enumerate(offsets):
            for right_index, right in enumerate(offsets):
                if (left + right) % total_rows == target:
                    entries.append((left_index, right_index))
        by_target.append(entries)
    return by_target


def runs_of(indices):
    runs = []
    for position, index in enumerate(indices):
        if runs and runs[-1][1] + runs[-1][2] == index:
            runs[-1][2] += 1
        else:
            runs.append([position, index, 1])
    return runs


def pieces_of(low, high, local_rows):
    for ahead in range(low // local_rows, (high - 1) // local_rows + 1):
        first = max(low, ahead * local_rows)
        last = min(high, (ahead + 1) * local_rows)
        yield ahead, first - ahead * local_rows, last - first, first - low


def kernel(sizes, needed, by_target, tiles, presence, out, near, ahead_far, behind_far, squared, done,
           send_sem, near_sem, ahead_sem, behind_sem, out_send_sem, out_sem):
    groups, columns, layers, local_rows, rows, part, size = sizes
    me_layer = lax.axis_index("layer")
    me_group = lax.axis_index("row") * columns + lax.axis_index("col")

    def device(steps, layer):
        group = lax.rem(me_group + steps % groups, groups)
        return {"row": lax.div(group, columns), "col": lax.rem(group, columns), "layer": layer}

    everything = list(range(len(by_target)))
    windows = [
        (near, near_sem, -BAND, rows + BAND, everything),
        (ahead_far, ahead_sem, FAR - 1, rows + FAR + 1, needed[0]),
        (behind_far, behind_sem, -FAR - 1, rows - FAR + 1, needed[1]),
    ]
    my_part = pl.ds(pl.multiple_of(me_layer * part, part), part)

    def each_copy(act_remote, act_local):
        for window, sem, low, high, diagonals in windows:
            for layer in range(layers):
                for steps, source_row, count, window_row in pieces_of(
                    low + layer * rows, high + layer * rows, local_rows
                ):
                    for position, index, length in runs_of(diagonals):
                        source = tiles.at[pl.ds(index, length), pl.ds(source_row, count)]
                        target = window.at[pl.ds(position, length), pl.ds(window_row, count), my_part]

                        def remote():
                            act_remote(
                                pltpu.make_async_remote_copy(
                                    src_ref=source, dst_ref=target, send_sem=send_sem, recv_sem=sem,
                                    device_id=device(-steps, layer), device_id_type=MESH,
                                )
                            )

                        def local():
                            if act_local is not None:
                                act_local(pltpu.make_async_copy(source, target, sem))

                        if steps % groups == 0:
                            pl.when(me_layer != layer)(remote)
                            pl.when(me_layer == layer)(local)
                        else:
                            remote()

    each_copy(lambda copy: copy.start(), lambda copy: copy.start())
    each_copy(lambda copy: copy.wait_send(), None)
    for window, sem, *_ in windows:
        pltpu.make_async_copy(window, window, sem).wait()

    def right_tile(left, right, row):
        if left < WIDTH:
            return near[right, row + left]
        if left < WIDTH + 3:
            return ahead_far[needed[0].index(right), row + left - WIDTH]
        return behind_far[needed[1].index(right), row + left - WIDTH - 3]

    couples = [(0, 1), (2, 3), (4, 5), (6,), (7, 8), (9,), (10, 11), (12,)]

    def product(left_tile, row, finish):
        for couple in couples:
            tables = [dict(by_target[target]) for target in couple]
            lefts = sorted(set(left for table in tables for left in table))
            lhs = jnp.concatenate([left_tile(left) for left in lefts], axis=1)
            rhs = jnp.concatenate(
                [
                    jnp.concatenate(
                        [
                            right_tile(left, table[left], row)
                            if left in table
                            else jnp.zeros((size, size), jnp.bfloat16)
                            for table in tables
                        ],
                        axis=1,
                    )
                    for left in lefts
                ],
                axis=0,
            )
            total = jnp.dot(lhs, rhs, preferred_element_type=jnp.float32)
            for place, target in enumerate(couple):
                finish(target, total[:, place * size : (place + 1) * size])

    def each_result(row, act_remote, act_local):
        place = me_layer * rows + row
        for layer in range(layers):
            source = done.at[row, :, pl.ds(layer * part, part)]
            target = out.at[:, place]

            def remote():
                act_remote(
                    pltpu.make_async_remote_copy(
                        src_ref=source, dst_ref=target, send_sem=out_send_sem, recv_sem=out_sem,
                        device_id=device(0, layer), device_id_type=MESH,
                    )
                )

            def local():
                if act_local is not None:
                    act_local(pltpu.make_async_copy(source, target, out_sem))

            pl.when(me_layer != layer)(remote)
            pl.when(me_layer == layer)(local)

    def start(copy):
        copy.start()

    @pl.loop(0, rows)
    def _(row):
        def weight(target):
            return presence[target, me_layer * rows + row].astype(jnp.float32)

        def store_square(target, total):
            squared[target] = (total * weight(target)).astype(jnp.bfloat16)

        def store_result(target, total):
            third = total * weight(target)
            done[row, target] = (3.0 * squared[target].astype(jnp.float32) - 2.0 * third).astype(jnp.bfloat16)

        product(lambda left: near[left, row + BAND], row, store_square)
        product(lambda left: squared[left], row, store_result)

        @pl.when(row > 0)
        def _():
            each_result(row - 1, start, start)

    each_result(rows - 1, start, start)

    @pl.loop(0, rows)
    def _(row):
        each_result(row, lambda copy: copy.wait_send(), None)

    pltpu.make_async_copy(out, out, out_sem).wait()


def solution(mesh):
    columns = mesh.shape["col"]
    layers = mesh.shape["layer"]
    groups = mesh.shape["row"] * columns

    def per_device(blocks, presence):
        diagonals, local_rows, part, size = blocks.shape
        total_rows = local_rows * groups
        rows = local_rows // layers
        offsets = offset_table(total_rows)
        by_target = pair_table(offsets, total_rows)
        needed = []
        for first in (WIDTH, WIDTH + 3):
            lefts = range(first, first + 3)
            needed.append(sorted(set(b for pairs in by_target for a, b in pairs if a in lefts)))
        masked = blocks * presence.astype(jnp.bfloat16)[:, :, None, None]
        sizes = (groups, columns, layers, local_rows, rows, part, size)
        return pl.pallas_call(
            functools.partial(kernel, sizes, needed, by_target),
            out_shape=jax.ShapeDtypeStruct(blocks.shape, jnp.bfloat16),
            in_specs=[pl.BlockSpec(memory_space=pl.ANY), pl.BlockSpec(memory_space=pltpu.SMEM)],
            out_specs=pl.BlockSpec(memory_space=pl.ANY),
            scratch_shapes=[
                pltpu.VMEM((diagonals, rows + 2 * BAND, size, size), jnp.bfloat16),
                pltpu.VMEM((len(needed[0]), rows + 2, size, size), jnp.bfloat16),
                pltpu.VMEM((len(needed[1]), rows + 2, size, size), jnp.bfloat16),
                pltpu.VMEM((diagonals, size, size), jnp.bfloat16),
                pltpu.VMEM((rows, diagonals, size, size), jnp.bfloat16),
            ]
            + [pltpu.SemaphoreType.DMA] * 6,
            compiler_params=pltpu.CompilerParams(has_side_effects=True, vmem_limit_bytes=48 * 2**20),
        )(masked, presence)

    return jax.shard_map(
        per_device,
        mesh=mesh,
        in_specs=(P(None, ("row", "col"), "layer", None), P(None, ("row", "col"))),
        out_specs=P(None, ("row", "col"), "layer", None),
        check_vma=False,
    )
```

time: 2250 us -> 515 us (0.23)
  waiting for transfers between devices: 1060 us -> 0 us
  local copies, waits for them, and re-layouts: 707 us -> 7.12 us
  Pallas kernels: 0 us -> 500 us
  starting transfers between devices: 179 us -> 0 us
  matrix products: 136 us -> 0 us
  blocking collectives: 83.3 us -> 0 us
  other arithmetic: 49.6 us -> 7.29 us
    reduce_scatter x2 -> x0, waiting for transfers between devices: 696 us -> none  [the longest x1 457 us: per_device(): lax.psum_scatter(product(left_first), 'layer', scatter_dimension=2, tiled...]
    pallas_call x0 -> x1, Pallas kernels: none -> 500 us  [per_device(): pl.pallas_call(functools.partial(kernel, sizes, needed, by_target), out_s...]
    concatenate x30 -> x0, local copies, waits for them, and re-layouts: 369 us -> none  [the longest x22 359 us: product(): jnp.concatenate([left_tiles[left_index] for left_index, right_index in pa...]
    ppermute x14 -> x0, waiting for transfers between devices: 367 us -> none  [the longest x12 367 us: passed_along(): return lax.ppermute(block, axis, route)]
    ppermute x14 -> x0, starting transfers between devices: 174 us -> none  [the longest x12 169 us: passed_along(): return lax.ppermute(block, axis, route)]
    slice x39 -> x0, local copies, waits for them, and re-layouts: 155 us -> none  [the longest x28 134 us: product(): left_tiles[left_index]]
    dot_general x26 -> x0, matrix products: 136 us -> none  [product(): jnp.einsum('ixk,iky->ixy', lefts, rights, preferred_element_type=jnp.floa...]
    all_to_all x1 -> x0, blocking collectives: 83.3 us -> none  [per_device(): lax.all_to_all(second, 'layer', split_axis=3, concat_axis=2, tiled=True)]
  transfers between devices with their start and end apart: 17 -> 0, of which waited for: 7 -> 0; matrix products, arithmetic and copies ran while one was open for 5% -> 0% of each run, Pallas kernels for 0% -> 0%
where the time goes in v1:
time: 515 us
  Pallas kernels  500 us (97%)
  other arithmetic  7.29 us (1%)
  local copies, waits for them, and re-layouts  7.12 us (1%)
    pallas_call x1, Pallas kernels, per_device(): pl.pallas_call(functools.partial(kernel, sizes, needed, by_target), out_s...  500 us

profile of v1, /device:TPU:0, one launch (start us, length us, event | category | flops | bytes accessed | tf_op | source)
XLA Modules:
  0.0 514.7 jit_solution(7490107120252297684)
XLA Ops:
  0.0 0.7 convert_element_type.3
  0.7 0.0 copy-start
  0.7 6.6 %broadcast_multiply_fusion.tiles = bf16[13,64,32,128]{3,2,1,0:T(8,128)(2,1)} fusion(bf16[13,64,32,128]{3,2,1,0:T(8,128)(2,1)} %param.2, bf16[13,64]{1,0:T(8,128)(2,1)S(1)} %convert_element_type.3), kind=kLoop, calls=%fused_computation | loop fusion | flops 3407872 | bytes 13633152 | tf_op jit(solution)/shard_map/mul | solution.py:202
  7.3 0.0 copy-done
  7.3 500.3 %shard_map.28 = bf16[13,64,32,128]{3,2,1,0:T(8,128)(2,1)} custom-call(bf16[13,64,32,128]{3,2,1,0:T(8,128)(2,1)} %broadcast_multiply_fusion.tiles, s32[13,64]{1,0:T(8,128)S(1)} %copy-done), custom_call_target="tpu_custom_call" | custom-call | tf_op jit(solution)/shard_map/pallas_call | solution.py:204
  507.6 7.1 %copy.4 = bf16[13,64,32,128]{3,2,1,0:T(8,128)(2,1)} copy(bf16[13,64,32,128]{3,2,1,0:T(8,128)(2,1)} %shard_map.28) | data formatting | bytes 13631488
Async XLA Ops:
  0.7 6.6 %copy-start = (s32[13,64]{1,0:T(8,128)S(1)}, s32[13,64]{1,0:T(8,128)}, u32[]{:S(2)}) copy-start(s32[13,64]{1,0:T(8,128)} %presence.1) | copy-start | bytes 9988

commit v2 on v1

--- a/solution.py
+++ b/solution.py
@@ -9,6 +9,7 @@
 
 BAND = 3
 FAR = 160
+CHUNKS = 4
 WIDTH = 2 * BAND + 1
 MESH = pl.DeviceIdType.MESH
 
@@ -60,51 +61,72 @@
 
     everything = list(range(len(by_target)))
     windows = [
-        (near, near_sem, -BAND, rows + BAND, everything),
-        (ahead_far, ahead_sem, FAR - 1, rows + FAR + 1, needed[0]),
-        (behind_far, behind_sem, -FAR - 1, rows - FAR + 1, needed[1]),
+        (near, near_sem, -BAND, 2 * BAND, everything),
+        (ahead_far, ahead_sem, FAR - 1, 2, needed[0]),
+        (behind_far, behind_sem, -FAR - 1, 2, needed[1]),
     ]
-    my_part = pl.ds(pl.multiple_of(me_layer * part, part), part)
-
-    def each_copy(act_remote, act_local):
-        for window, sem, low, high, diagonals in windows:
+    chunks = CHUNKS if rows % CHUNKS == 0 else rows
+    step_rows = rows // chunks
+
+    def chunk_rows(chunk, extra):
+        first = 0 if chunk == 0 else chunk * step_rows + extra
+        return first, (chunk + 1) * step_rows + extra
+
+    def copies_to(chunk, layer, act_remote, act_local):
+        for window, sem, low, extra, diagonals in windows:
+            first, last = chunk_rows(chunk, extra)
+            start_row = low + layer * rows
+            for steps, source_row, count, window_row in pieces_of(
+                start_row + first, start_row + last, local_rows
+            ):
+                for position, index, length in runs_of(diagonals):
+                    source = tiles.at[pl.ds(index, length), pl.ds(source_row, count)]
+                    target = window.at[me_layer, pl.ds(position, length), pl.ds(first + window_row, count)]
+
+                    def remote():
+                        act_remote(
+                            pltpu.make_async_remote_copy(
+                                src_ref=source, dst_ref=target, send_sem=send_sem, recv_sem=sem.at[chunk],
+                                device_id=device(-steps, layer), device_id_type=MESH,
+                            )
+                        )
+
+                    def local():
+                        if act_local is not None:
+                            act_local(pltpu.make_async_copy(source, target, sem.at[chunk]))
+
+                    if steps % groups == 0:
+                        pl.when(me_layer != layer)(remote)
+                        pl.when(me_layer == layer)(local)
+                    else:
+                        remote()
+
+    def start(copy):
+        copy.start()
+
+    for chunk in range(chunks):
+        for turn in range(layers):
             for layer in range(layers):
-                for steps, source_row, count, window_row in pieces_of(
-                    low + layer * rows, high + layer * rows, local_rows
-                ):
-                    for position, index, length in runs_of(diagonals):
-                        source = tiles.at[pl.ds(index, length), pl.ds(source_row, count)]
-                        target = window.at[pl.ds(position, length), pl.ds(window_row, count), my_part]
-
-                        def remote():
-                            act_remote(
-                                pltpu.make_async_remote_copy(
-                                    src_ref=source, dst_ref=target, send_sem=send_sem, recv_sem=sem,
-                                    device_id=device(-steps, layer), device_id_type=MESH,
-                                )
-                            )
-
-                        def local():
-                            if act_local is not None:
-                                act_local(pltpu.make_async_copy(source, target, sem))
-
-                        if steps % groups == 0:
-                            pl.when(me_layer != layer)(remote)
-                            pl.when(me_layer == layer)(local)
-                        else:
-                            remote()
-
-    each_copy(lambda copy: copy.start(), lambda copy: copy.start())
-    each_copy(lambda copy: copy.wait_send(), None)
-    for window, sem, *_ in windows:
-        pltpu.make_async_copy(window, window, sem).wait()
+
+                @pl.when(lax.rem(me_layer + turn, layers) == layer)
+                def _():
+                    copies_to(chunk, layer, start, start)
+
+    def wait_for(chunk):
+        for window, sem, _, extra, _ in windows:
+            first, last = chunk_rows(chunk, extra)
+            arrived = window.at[:, :, pl.ds(first, last - first)]
+            pltpu.make_async_copy(arrived, arrived, sem.at[chunk]).wait()
+
+    def tile_of(window, index, row):
+        return jnp.concatenate([window[layer, index, row] for layer in range(layers)], axis=0)
 
     def right_tile(left, right, row):
         if left < WIDTH:
-            return near[right, row + left]
+            return tile_of(near, right, row + left)
         if left < WIDTH + 3:
-            return ahead_far[needed[0].index(right), row + left - WIDTH]
-        return behind_far[needed[1].index(right), row + left - WIDTH - 3]
+            return tile_of(ahead_far, needed[0].index(right), row + left - WIDTH)
+        return tile_of(behind_far, needed[1].index(right), row + left - WIDTH - 3)
 
     couples = [(0, 1), (2, 3), (4, 5), (6,), (7, 8), (9,), (10, 11), (12,)]
 
@@ -135,7 +157,7 @@
     def each_result(row, act_remote, act_local):
         place = me_layer * rows + row
         for layer in range(layers):
-            source = done.at[row, :, pl.ds(layer * part, part)]
+            source = done.at[row, layer]
             target = out.at[:, place]
 
             def remote():
@@ -153,11 +175,14 @@
             pl.when(me_layer != layer)(remote)
             pl.when(me_layer == layer)(local)
 
-    def start(copy):
-        copy.start()
-
     @pl.loop(0, rows)
     def _(row):
+        for chunk in range(chunks):
+
+            @pl.when(row == chunk * step_rows)
+            def _():
+                wait_for(chunk)
+
         def weight(target):
             return presence[target, me_layer * rows + row].astype(jnp.float32)
 
@@ -166,9 +191,11 @@
 
         def store_result(target, total):
             third = total * weight(target)
-            done[row, target] = (3.0 * squared[target].astype(jnp.float32) - 2.0 * third).astype(jnp.bfloat16)
-
-        product(lambda left: near[left, row + BAND], row, store_square)
+            result = (3.0 * squared[target].astype(jnp.float32) - 2.0 * third).astype(jnp.bfloat16)
+            for layer in range(layers):
+                done[row, layer, target] = result[layer * part : (layer + 1) * part]
+
+        product(lambda left: tile_of(near, left, row + BAND), row, store_square)
         product(lambda left: squared[left], row, store_result)
 
         @pl.when(row > 0)
@@ -176,6 +203,9 @@
             each_result(row - 1, start, start)
 
     each_result(rows - 1, start, start)
+    for chunk in range(chunks):
+        for layer in range(layers):
+            copies_to(chunk, layer, lambda copy: copy.wait_send(), None)
 
     @pl.loop(0, rows)
     def _(row):
@@ -207,13 +237,18 @@
             in_specs=[pl.BlockSpec(memory_space=pl.ANY), pl.BlockSpec(memory_space=pltpu.SMEM)],
             out_specs=pl.BlockSpec(memory_space=pl.ANY),
             scratch_shapes=[
-                pltpu.VMEM((diagonals, rows + 2 * BAND, size, size), jnp.bfloat16),
-                pltpu.VMEM((len(needed[0]), rows + 2, size, size), jnp.bfloat16),
-                pltpu.VMEM((len(needed[1]), rows + 2, size, size), jnp.bfloat16),
+                pltpu.VMEM((layers, diagonals, rows + 2 * BAND, part, size), jnp.bfloat16),
+                pltpu.VMEM((layers, len(needed[0]), rows + 2, part, size), jnp.bfloat16),
+                pltpu.VMEM((layers, len(needed[1]), rows + 2, part, size), jnp.bfloat16),
                 pltpu.VMEM((diagonals, size, size), jnp.bfloat16),
-                pltpu.VMEM((rows, diagonals, size, size), jnp.bfloat16),
-            ]
-            + [pltpu.SemaphoreType.DMA] * 6,
+                pltpu.VMEM((rows, layers, diagonals, part, size), jnp.bfloat16),
+                pltpu.SemaphoreType.DMA,
+                pltpu.SemaphoreType.DMA((rows,)),
+                pltpu.SemaphoreType.DMA((rows,)),
+                pltpu.SemaphoreType.DMA((rows,)),
+                pltpu.SemaphoreType.DMA,
+                pltpu.SemaphoreType.DMA,
+            ],
             compiler_params=pltpu.CompilerParams(has_side_effects=True, vmem_limit_bytes=48 * 2**20),
         )(masked, presence)
 

time: 515 us -> 397 us (0.77)
  the two profiles are of different devices: /device:TPU:0 before, /device:TPU:30 now
where the time goes in v2:
time: 397 us
  Pallas kernels  383 us (96%)
  other arithmetic  7.29 us (2%)
  local copies, waits for them, and re-layouts  7.12 us (2%)
    pallas_call x1, Pallas kernels, per_device(): pl.pallas_call(functools.partial(kernel, sizes, needed, by_target), out_s...  383 us

profile of v2, /device:TPU:30, one launch (start us, length us, event | category | flops | bytes accessed | tf_op | source)
XLA Modules:
  0.0 396.9 jit_solution(11667079950006123488)
XLA Ops:
  0.0 0.7 convert_element_type.3
  0.7 0.0 copy-start
  0.7 6.6 %broadcast_multiply_fusion.tiles = bf16[13,64,32,128]{3,2,1,0:T(8,128)(2,1)} fusion(bf16[13,64,32,128]{3,2,1,0:T(8,128)(2,1)} %param.2, bf16[13,64]{1,0:T(8,128)(2,1)S(1)} %convert_element_type.3), kind=kLoop, calls=%fused_computation | loop fusion | flops 3407872 | bytes 13633152 | tf_op jit(solution)/shard_map/mul | solution.py:232
  7.3 0.0 copy-done
  7.3 382.5 %shard_map.28 = bf16[13,64,32,128]{3,2,1,0:T(8,128)(2,1)} custom-call(bf16[13,64,32,128]{3,2,1,0:T(8,128)(2,1)} %broadcast_multiply_fusion.tiles, s32[13,64]{1,0:T(8,128)S(1)} %copy-done), custom_call_target="tpu_custom_call" | custom-call | tf_op jit(solution)/shard_map/pallas_call | solution.py:234
  389.8 7.1 %copy.4 = bf16[13,64,32,128]{3,2,1,0:T(8,128)(2,1)} copy(bf16[13,64,32,128]{3,2,1,0:T(8,128)(2,1)} %shard_map.28) | data formatting | bytes 13631488
Async XLA Ops:
  0.7 6.6 %copy-start = (s32[13,64]{1,0:T(8,128)S(1)}, s32[13,64]{1,0:T(8,128)}, u32[]{:S(2)}) copy-start(s32[13,64]{1,0:T(8,128)} %presence.1) | copy-start | bytes 9988

commit v3 on v2

--- a/solution.py
+++ b/solution.py
@@ -9,7 +9,7 @@
 
 BAND = 3
 FAR = 160
-CHUNKS = 4
+CHUNKS = 8
 WIDTH = 2 * BAND + 1
 MESH = pl.DeviceIdType.MESH
 

time: 397 us -> 371 us (0.935)
  the two profiles are of different devices: /device:TPU:30 before, /device:TPU:0 now
where the time goes in v3:
time: 371 us; the launch traced here: 366 us
  Pallas kernels  352 us (95%)
  other arithmetic  7.29 us (2%)
  local copies, waits for them, and re-layouts  7.12 us (2%)
    pallas_call x1, Pallas kernels, per_device(): pl.pallas_call(functools.partial(kernel, sizes, needed, by_target), out_s...  352 us

profile of v3, /device:TPU:0, one launch (start us, length us, event | category | flops | bytes accessed | tf_op | source)
XLA Modules:
  0.0 366.5 jit_solution(14251864586016316982)
XLA Ops:
  0.0 0.7 convert_element_type.3
  0.7 0.0 copy-start
  0.7 6.6 %broadcast_multiply_fusion.tiles = bf16[13,64,32,128]{3,2,1,0:T(8,128)(2,1)} fusion(bf16[13,64,32,128]{3,2,1,0:T(8,128)(2,1)} %param.2, bf16[13,64]{1,0:T(8,128)(2,1)S(1)} %convert_element_type.3), kind=kLoop, calls=%fused_computation | loop fusion | flops 3407872 | bytes 13633152 | tf_op jit(solution)/shard_map/mul | solution.py:232
  7.3 0.0 copy-done
  7.3 352.0 %shard_map.28 = bf16[13,64,32,128]{3,2,1,0:T(8,128)(2,1)} custom-call(bf16[13,64,32,128]{3,2,1,0:T(8,128)(2,1)} %broadcast_multiply_fusion.tiles, s32[13,64]{1,0:T(8,128)S(1)} %copy-done), custom_call_target="tpu_custom_call" | custom-call | tf_op jit(solution)/shard_map/pallas_call | solution.py:234
  359.3 7.1 %copy.4 = bf16[13,64,32,128]{3,2,1,0:T(8,128)(2,1)} copy(bf16[13,64,32,128]{3,2,1,0:T(8,128)(2,1)} %shard_map.28) | data formatting | bytes 13631488
Async XLA Ops:
  0.7 6.6 %copy-start = (s32[13,64]{1,0:T(8,128)S(1)}, s32[13,64]{1,0:T(8,128)}, u32[]{:S(2)}) copy-start(s32[13,64]{1,0:T(8,128)} %presence.1) | copy-start | bytes 9988
